TPU v7x, 128 devices: a whole 4x4x4 slice. The times are simulated.
128 devices in a mesh: pts: 16 (over z, y), hrs: 8 (over x, core).
Axes of the slice: x: 4, y: 4, z: 4, core: 2. Of those that a mesh axis runs over, the one named last changes fastest.
Arguments:
- fields: float32 [512, 262144], P(('pts', 'hrs')), may hold values from -2000 to 2000, as said below
- probes: float32 [256, 512], replicated, may hold values from -0.25 to 0.25
Outputs:
- basis_rows: float32 [256, 262144], P(None, ('pts', 'hrs'))
- coeffs: float32 [256, 512], replicated
Inputs may be any that keep to these rules, and one draw needn't show every extreme that they name: `fields`: every hour and every grid point carries its own scale, and the values are real-valued and never all zero.
All inputs are finite; a program needn't handle non-finite values.
Results may differ from a plain program's by a relative error of at most 0.00017.
Values sent between devices are 32-bit elements; how exact they have to be, the bound alone decides.
No kernel may reach another device: no remote copies, remote signals or barrier semaphores. Data moves between devices by JAX's collectives and lax.ppermute only.
A program may use at most 64 MiB of HBM per device.

v0:
```python
import jax
import jax.numpy as jnp
from jax import lax
from jax.sharding import PartitionSpec as P

highest = lax.Precision.HIGHEST


def contract_last(left, right):
    return lax.dot_general(
        left, right, (((1,), (1,)), ((), ())), precision=highest, preferred_element_type=jnp.float32
    )


def on_device(fields, probes):
    n_pts = lax.axis_size("pts")
    n_hrs = lax.axis_size("hrs")
    panels = lax.all_to_all(fields, ("pts", "hrs"), split_axis=1, concat_axis=0, tiled=True)
    n_points = panels.shape[1] * n_pts * n_hrs
    sketched = jnp.dot(probes, panels, precision=highest, preferred_element_type=jnp.float32)
    local_gram = contract_last(sketched, sketched) / n_points
    gram_sum = lax.psum(local_gram, ("pts", "hrs"))
    factor = jnp.linalg.cholesky(gram_sum)
    basis_rows = lax.linalg.triangular_solve(factor, sketched, left_side=True, lower=True)
    coeffs = lax.psum(contract_last(basis_rows, panels) / n_points, ("pts", "hrs"))
    return (basis_rows, coeffs)


def solution(mesh):
    return jax.shard_map(
        on_device,
        mesh=mesh,
        in_specs=(P(("pts", "hrs"), None), P()),
        out_specs=(P(None, ("pts", "hrs")), P()),
        check_vma=False,
    )
```

profile of v0, /device:TPU:1, one launch (start us, length us, event | category | flops | bytes accessed | tf_op | source)
XLA Modules:
  0.0 445.6 jit_solution(2200279935162737825)
XLA Ops:
  7.2 0.0 all-reduce.4.cloned.1.call-start
  7.2 64.6 %all_to_all.19 = f32[4,128,2048]{2,0,1:T(4,128)} all-to-all(f32[4,128,2048]{2,0,1:T(4,128)} %bitcast.40), channel_id=1, replica_groups=mesh['pts'=16,'hrs'=8] {'pts','hrs'}, dimensions={1} | all-to-all | bytes 8388608 | tf_op jit(solution)/shard_map/all_to_all | solution.py:18
  71.8 5.3 %all_to_all.17 = f32[512,2048]{1,0:T(8,128)} reshape(f32[128,4,2048]{2,1,0:T(4,128)} %bitcast.39) | data formatting | bytes 8388608 | tf_op jit(solution)/shard_map/all_to_all | solution.py:18
  77.1 5.4 %fusion.9 = f32[256,2048]{1,0:T(8,128)S(1)} fusion(f32[256,512]{1,0:T(8,128)S(1)} %copy-done, f32[512,2048]{1,0:T(8,128)} %all_to_all.17), kind=kOutput, calls=%fused_computation.31 | convolution fusion | flops 3221225472 | bytes 6815744 | tf_op jit(solution)/shard_map/dot_general | solution.py:20
  82.6 2.6 convolution_multiply_fusion.1
  85.1 0.0 all-reduce.4.cloned.1.call-update
  85.1 0.2 all-reduce.6.cloned.1.call-start
  85.4 137.0 %all-reduce.4.cloned.1.call-done = f32[256,256]{0,1:T(8,128)} async-done(((f32[256,256]{0,1:T(8,128)}), f32[256,256]{0,1:T(8,128)}) %all-reduce.4.cloned.1.call-update) | async-done | bytes 262160 | tf_op jit(solution)/shard_map/psum | solution.py:22
  222.4 1.1 copy.8
  223.5 1.0 fusion.2
  224.5 11.7 %cholesky.50 = f32[128,128]{1,0:T(8,128)S(1)} custom-call(f32[128,128]{1,0:T(8,128)S(1)} %cholesky.118), custom_call_target="Cholesky" | custom-call | tf_op jit(solution)/shard_map/jit(cholesky)/cholesky | solution.py:23
  236.2 9.8 %custom-call.14 = f32[1,128,128]{1,2,0:T(8,128)S(1)} custom-call(f32[1,128,128]{2,1,0:T(8,128)S(1)} %get-tuple-element.23), custom_call_target="InvertDiagBlocksLowerTriangular" | custom-call | tf_op jit(solution)/shard_map/jit(cholesky)/cholesky | solution.py:23
  246.1 0.2 constant_dynamic-update-slice_fusion.1
  246.3 0.3 convolution_subtract_fusion.1
  246.6 11.7 %cholesky.105 = f32[128,128]{1,0:T(8,128)S(1)} custom-call(f32[128,128]{1,0:T(8,128)S(1)} %convolution_subtract_fusion.1), custom_call_target="Cholesky" | custom-call | tf_op jit(solution)/shard_map/jit(cholesky)/cholesky | solution.py:23
  258.3 0.7 compare_reduce_fusion
  260.3 0.1 triangular_solve.57
  260.4 4.1 while.1
  260.5 0.6 fusion.21
  261.1 1.4 bitcast_dynamic-update-slice_fusion.2
  262.5 0.6 fusion.21
  263.1 1.4 bitcast_dynamic-update-slice_fusion.2
  264.5 19.7 %custom-call.15 = f32[2,128,128]{1,2,0:T(8,128)S(1)} custom-call(f32[2,128,128]{2,1,0:T(8,128)S(1)} %get-tuple-element.9), custom_call_target="InvertDiagBlocksLowerTriangular" | custom-call | tf_op jit(solution)/shard_map/triangular_solve | solution.py:24
  284.1 1.1 fusion
  285.2 1.0 convolution_subtract_fusion
  286.2 1.1 fusion.4
  287.3 0.1 pad_maximum_fusion
  287.4 2.0 copy-done.1
  289.5 4.5 %convolution_multiply_fusion = f32[256,512]{1,0:T(8,128)} fusion(f32[256,2048]{1,0:T(8,128)S(1)} %pad_maximum_fusion, f32[512,2048]{1,0:T(8,128)S(1)} %copy-done.1), kind=kOutput, calls=%fused_computation.4 | convolution fusion | flops 3221356544 | bytes 6815744 | tf_op jit(solution)/shard_map/dot_general | solution.py:10
  294.0 0.0 all-reduce.6.cloned.1.call-update
  294.0 142.8 %all-reduce.6.cloned.1.call-done = f32[256,512]{1,0:T(8,128)} async-done(((f32[256,512]{1,0:T(8,128)}), f32[256,512]{1,0:T(8,128)}) %all-reduce.6.cloned.1.call-update) | async-done | bytes 524304 | tf_op jit(solution)/shard_map/psum | solution.py:25
  436.9 1.9 copy.23
  (14 shorter events, 0.2 us)
Async XLA Ops:
  7.2 70.0 %copy-start = (f32[256,512]{1,0:T(8,128)S(1)}, f32[256,512]{1,0:T(8,128)}, u32[]{:S(2)}) copy-start(f32[256,512]{1,0:T(8,128)} %param.3) | copy-start | bytes 1572868
  7.2 215.2 %all-reduce.4.cloned.1.call-start = ((), (), s32[]{:S(2)}) async-start(), calls=%async_computation.1 | async-start | bytes 524288 | tf_op jit(solution)/shard_map/psum | solution.py:22
  85.1 351.7 %all-reduce.6.cloned.1.call-start = ((), (), s32[]{:S(2)}) async-start(), calls=%async_computation.2 | async-start | bytes 1048576 | tf_op jit(solution)/shard_map/psum | solution.py:25
  287.3 2.2 copy-start.1
  289.5 4.5 %copy-start.2 = (f32[256,2048]{1,0:T(8,128)}, f32[256,2048]{1,0:T(8,128)S(1)}, u32[]{:S(2)}) copy-start(f32[256,2048]{1,0:T(8,128)S(1)} %pad_maximum_fusion) | copy-start | bytes 6291460
Sparse Core Ops, SparseCore 0:
  85.3 137.0 all-reduce.3
  294.1 142.6 all-reduce.5
where the time goes:
time: 446 us
  waiting for transfers between devices  280 us (63%)
  blocking collectives  64.6 us (14%)
  other arithmetic  54.8 us (12%)
  matrix products  16.1 us (4%)
  between operations  15.4 us (3%)
  local copies, waits for them, and re-layouts  14.3 us (3%)
    psum x1, waiting for transfers between devices, on_device(): lax.psum(contract_last(basis_rows, panels) / n_points, ('pts', 'hrs'))  143 us
    psum x1, waiting for transfers between devices, on_device(): gram_sum = lax.psum(local_gram, ('pts', 'hrs'))  137 us
    all_to_all x1, blocking collectives, on_device(): lax.all_to_all(fields, ('pts', 'hrs'), split_axis=1, concat_axis=0, tiled...  64.6 us
    another operation x6, other arithmetic, on_device(): factor = jnp.linalg.cholesky(gram_sum)  34 us
    another operation x4, other arithmetic, on_device(): lax.linalg.triangular_solve(factor, sketched, left_side=True, lower=True)  19.9 us
  transfers between devices with their start and end apart: 2, of which 2 were waited for; matrix products, arithmetic and copies ran while one was open for 0% of the time, Pallas kernels for 0%

commit v1 on v0

--- a/solution.py
+++ b/solution.py
@@ -19,7 +19,8 @@
     n_points = panels.shape[1] * n_pts * n_hrs
     sketched = jnp.dot(probes, panels, precision=highest, preferred_element_type=jnp.float32)
     local_gram = contract_last(sketched, sketched) / n_points
-    gram_sum = lax.psum(local_gram, ("pts", "hrs"))
+    parts = lax.all_gather(local_gram, ("pts", "hrs"))
+    gram_sum = jnp.sum(parts, axis=0)
     factor = jnp.linalg.cholesky(gram_sum)
     basis_rows = lax.linalg.triangular_solve(factor, sketched, left_side=True, lower=True)
     coeffs = lax.psum(contract_last(basis_rows, panels) / n_points, ("pts", "hrs"))

time: 446 us -> 424 us (0.951)
  waiting for transfers between devices: 280 us -> 247 us
  other arithmetic: 54.8 us -> 66.1 us
    psum x1 -> x0, waiting for transfers between devices: 137 us -> none  [on_device(): gram_sum = lax.psum(local_gram, ('pts', 'hrs'))]
    all_gather x0 -> x1, waiting for transfers between devices: none -> 103 us  [on_device(): parts = lax.all_gather(local_gram, ('pts', 'hrs'))]
    reduce_sum x0 -> x1, other arithmetic: none -> 12 us  [on_device(): gram_sum = jnp.sum(parts, axis=0)]
where the time goes in v1:
time: 424 us; the launch traced here: 423 us
  waiting for transfers between devices  247 us (58%)
  other arithmetic  66.1 us (16%)
  blocking collectives  64.6 us (15%)
  matrix products  16.1 us (4%)
  between operations  15.5 us (4%)
  local copies, waits for them, and re-layouts  13.5 us (3%)
    psum x1, waiting for transfers between devices, on_device(): lax.psum(contract_last(basis_rows, panels) / n_points, ('pts', 'hrs'))  144 us
    all_gather x1, waiting for transfers between devices, on_device(): parts = lax.all_gather(local_gram, ('pts', 'hrs'))  103 us
    all_to_all x1, blocking collectives, on_device(): lax.all_to_all(fields, ('pts', 'hrs'), split_axis=1, concat_axis=0, tiled...  64.6 us
    another operation x6, other arithmetic, on_device(): factor = jnp.linalg.cholesky(gram_sum)  34 us
    another operation x4, other arithmetic, on_device(): lax.linalg.triangular_solve(factor, sketched, left_side=True, lower=True)  20.1 us
    reduce_sum x1, other arithmetic, on_device(): gram_sum = jnp.sum(parts, axis=0)  12 us
  transfers between devices with their start and end apart: 2, of which 2 were waited for; matrix products, arithmetic and copies ran while one was open for 0% of the time, Pallas kernels for 0%

profile of v1, /device:TPU:1, one launch (start us, length us, event | category | flops | bytes accessed | tf_op | source)
XLA Modules:
  0.0 423.2 jit_solution(15242840674371165724)
XLA Ops:
  7.2 0.0 all-gather.3.cloned.1.call-start
  7.2 64.6 %all_to_all.19 = f32[4,128,2048]{2,0,1:T(4,128)} all-to-all(f32[4,128,2048]{2,0,1:T(4,128)} %bitcast.42), channel_id=1, replica_groups=mesh['pts'=16,'hrs'=8] {'pts','hrs'}, dimensions={1} | all-to-all | bytes 8388608 | tf_op jit(solution)/shard_map/all_to_all | solution.py:18
  71.8 5.3 %all_to_all.17 = f32[512,2048]{1,0:T(8,128)} reshape(f32[128,4,2048]{2,1,0:T(4,128)} %bitcast.41) | data formatting | bytes 8388608 | tf_op jit(solution)/shard_map/all_to_all | solution.py:18
  77.2 5.4 %fusion.9 = f32[256,2048]{1,0:T(8,128)S(1)} fusion(f32[256,512]{1,0:T(8,128)S(1)} %copy-done, f32[512,2048]{1,0:T(8,128)} %all_to_all.17), kind=kOutput, calls=%fused_computation.31 | convolution fusion | flops 3221225472 | bytes 6815744 | tf_op jit(solution)/shard_map/dot_general | solution.py:20
  82.6 2.6 convolution_multiply_fusion.1
  85.2 0.0 all-gather.3.cloned.1.call-update
  85.2 0.2 all-reduce.3.cloned.1.call-start
  85.4 102.6 %all-gather.3.cloned.1.call-done = f32[32768,256]{1,0:T(8,128)} async-done(((f32[256,256]{1,0:T(8,128)}), f32[32768,256]{1,0:T(8,128)}) %all-gather.3.cloned.1.call-update) | async-done | bytes 33554448 | tf_op jit(solution)/shard_map/all_gather | solution.py:22
  188.0 12.0 %reduce_sum.9 = f32[256,256]{1,0:T(8,128)S(1)} reduce(f32[128,256,256]{2,1,0:T(8,128)} %bitcast.40, f32[]{:T(128)} %constant.77.clone.1), dimensions={0}, to_apply=%region_0.0 | reduce | flops 8323072 | bytes 33816580 | tf_op jit(solution)/shard_map/reduce_sum | solution.py:23
  200.0 0.1 copy.8
  200.2 11.7 %cholesky.50 = f32[128,128]{1,0:T(8,128)S(1)} custom-call(f32[128,128]{1,0:T(8,128)S(1)} %cholesky.118), custom_call_target="Cholesky" | custom-call | tf_op jit(solution)/shard_map/jit(cholesky)/cholesky | solution.py:24
  212.0 9.8 %custom-call.14 = f32[1,128,128]{1,2,0:T(8,128)S(1)} custom-call(f32[1,128,128]{2,1,0:T(8,128)S(1)} %get-tuple-element.23), custom_call_target="InvertDiagBlocksLowerTriangular" | custom-call | tf_op jit(solution)/shard_map/jit(cholesky)/cholesky | solution.py:24
  221.8 0.2 constant_dynamic-update-slice_fusion.1
  222.0 0.3 convolution_subtract_fusion.1
  222.3 11.7 %cholesky.105 = f32[128,128]{1,0:T(8,128)S(1)} custom-call(f32[128,128]{1,0:T(8,128)S(1)} %convolution_subtract_fusion.1), custom_call_target="Cholesky" | custom-call | tf_op jit(solution)/shard_map/jit(cholesky)/cholesky | solution.py:24
  234.0 0.7 compare_reduce_fusion
  236.1 0.1 triangular_solve.57
  236.2 4.1 while.1
  236.2 0.6 fusion.21
  236.8 1.4 bitcast_dynamic-update-slice_fusion.2
  238.3 0.6 fusion.21
  238.9 1.4 bitcast_dynamic-update-slice_fusion.2
  240.3 19.9 %custom-call.15 = f32[2,128,128]{1,2,0:T(8,128)S(1)} custom-call(f32[2,128,128]{2,1,0:T(8,128)S(1)} %get-tuple-element.9), custom_call_target="InvertDiagBlocksLowerTriangular" | custom-call | tf_op jit(solution)/shard_map/triangular_solve | solution.py:25
  260.2 1.1 fusion
  261.3 1.0 convolution_subtract_fusion
  262.3 1.1 fusion.4
  263.4 0.1 pad_maximum_fusion
  263.5 2.0 copy-done.1
  265.5 4.5 %convolution_multiply_fusion = f32[256,512]{1,0:T(8,128)} fusion(f32[256,2048]{1,0:T(8,128)S(1)} %pad_maximum_fusion, f32[512,2048]{1,0:T(8,128)S(1)} %copy-done.1), kind=kOutput, calls=%fused_computation.4 | convolution fusion | flops 3221356544 | bytes 6815744 | tf_op jit(solution)/shard_map/dot_general | solution.py:10
  270.1 0.0 all-reduce.3.cloned.1.call-update
  270.1 144.4 %all-reduce.3.cloned.1.call-done = f32[256,512]{1,0:T(8,128)} async-done(((f32[256,512]{1,0:T(8,128)}), f32[256,512]{1,0:T(8,128)}) %all-reduce.3.cloned.1.call-update) | async-done | bytes 524304 | tf_op jit(solution)/shard_map/psum | solution.py:26
  414.5 1.9 copy.21
  (15 shorter events, 0.2 us)
Async XLA Ops:
  7.2 70.0 %copy-start = (f32[256,512]{1,0:T(8,128)S(1)}, f32[256,512]{1,0:T(8,128)}, u32[]{:S(2)}) copy-start(f32[256,512]{1,0:T(8,128)} %param.3) | copy-start | bytes 1572868
  7.2 180.9 %all-gather.3.cloned.1.call-start = ((), (), s32[]{:S(2)}) async-start(), calls=%async_computation.2 | async-start | bytes 33816576 | tf_op jit(solution)/shard_map/all_gather | solution.py:22
  85.2 329.3 %all-reduce.3.cloned.1.call-start = ((), (), s32[]{:S(2)}) async-start(), calls=%async_computation.1 | async-start | bytes 1048576 | tf_op jit(solution)/shard_map/psum | solution.py:26
  263.4 2.2 copy-start.1
  265.5 4.5 %copy-start.2 = (f32[256,2048]{1,0:T(8,128)}, f32[256,2048]{1,0:T(8,128)S(1)}, u32[]{:S(2)}) copy-start(f32[256,2048]{1,0:T(8,128)S(1)} %pad_maximum_fusion) | copy-start | bytes 6291460
Sparse Core Ops, SparseCore 0:
  85.3 102.6 all-gather.2
  270.2 144.2 all-reduce.2
